TPU v7x, 32 devices: a whole 2x2x4 slice. The times are simulated.
32 devices in a mesh: section: 2 (over x), dp: 16 (over z, y, core).
Axes of the slice: x: 2, y: 2, z: 4, core: 2. Of those that a mesh axis runs over, the one named last changes fastest.
Arguments:
- tokens_in: bfloat16 [3, 1024, 1024], P(None, 'dp'), may hold values from -6 to 6
- out_cotangent: bfloat16 [3, 1024, 1024], P(None, 'dp'), may hold values from -6 to 6
- in_weight: bfloat16 [2, 1024, 4384], P('section', 'dp'), may hold values from -0.1875 to 0.1875
- out_weight: bfloat16 [2, 2048, 1024], P('section', 'dp'), may hold values from -0.125 to 0.125
- norm_gain: float32 [2, 1024], P('section'), may hold values from 0.5 to 1.5
- conv_weight: float32 [2, 4, 2304], P('section'), may hold values from -3 to 3
- conv_bias: float32 [2, 2304], P('section'), may hold values from -3 to 3
- dt_bias: float32 [2, 32], P('section'), may hold values from -4 to 0
- a_log: float32 [2, 32], P('section'), may hold values from 0 to 2.77
- skip_gain: float32 [2, 32], P('section'), may hold values from 0.5 to 1.5
- gate_gain: float32 [2, 2048], P('section'), may hold values from 0.5 to 1.5
- group_fill: int32 [3, 32], P(None, 'dp'), may hold values from 0 to 32, as said below
- group_link: int32 [3, 32], P(None, 'dp'), may hold values from 0 to 1, as said below
Outputs:
- section_outputs: float32 [2, 3, 1024, 1024], P('section', None, 'dp')
- section_input_grads: float32 [2, 3, 1024, 1024], P('section', None, 'dp')
- grad_in_weight: float32 [2, 1024, 4384], P('section', 'dp')
- grad_out_weight: float32 [2, 2048, 1024], P('section', 'dp')
- grad_norm_gain: float32 [2, 1024], P('section')
- grad_conv_weight: float32 [2, 4, 2304], P('section')
- grad_conv_bias: float32 [2, 2304], P('section')
- grad_dt_bias: float32 [2, 32], P('section')
- grad_a_log: float32 [2, 32], P('section')
- grad_skip_gain: float32 [2, 32], P('section')
- grad_gate_gain: float32 [2, 2048], P('section')
Inputs may be any that keep to these rules, and one draw needn't show every extreme that they name: `group_fill`: each slot's groups hold whole sequences from the start of a group: a sequence fills groups, the last one from its start to its end, the rest of that group is unused; some groups are empty, and how many differs from slot to slot. Some group of every micro-batch is full. `group_link`: A link of 1 stands only on a group that is not the first of its slot, follows a full group and holds a token; every micro-batch has one.
All inputs are finite; a program needn't handle non-finite values.
Results may differ from a plain program's by a relative error of at most 0.0097.
Values may be sent and summed in bfloat16 or wider, within the bound.
No kernel may reach another device: no remote copies, remote signals or barrier semaphores. Data moves between devices by JAX's collectives and lax.ppermute only.
A program may use at most 128 MiB of HBM per device.

v0:
```python
import jax
import jax.numpy as jnp
from jax import lax
from jax.sharding import PartitionSpec as P

EPSILON = 1e-05
HIGHEST = lax.Precision.HIGHEST


def shifted_2(x, axis, by):
    peers = lax.axis_size(axis)
    pairs = [(i, i + by) for i in range(peers) if 0 <= i + by < peers]
    return lax.ppermute(x, axis, pairs)


def norm_map(values, gain_row):
    return (
        values * lax.rsqrt(jnp.mean(values * values, axis=-1, keepdims=True) + EPSILON) * gain_row
    )


def ssd_scan(x_heads, step_size, log_decay, input_b, input_c, link_row, groups):
    rows_all, head_count, head_size = x_heads.shape
    length = rows_all // groups
    state_size = input_b.shape[1]
    x_blocks = x_heads.reshape(groups, length, head_count, head_size)
    dt_blocks = step_size.reshape(groups, length, head_count)
    cumulative = jnp.cumsum(log_decay.reshape(groups, length, head_count), axis=1)
    b_blocks = input_b.reshape(groups, length, state_size)
    c_blocks = input_c.reshape(groups, length, state_size)
    scores = jnp.einsum("cin,cjn->cij", c_blocks, b_blocks, precision=HIGHEST)
    causal = jnp.arange(length)[:, None] >= jnp.arange(length)[None, :]
    decay_gap = cumulative[:, :, None, :] - cumulative[:, None, :, :]
    factors = jnp.exp(jnp.where(causal[None, :, :, None], decay_gap, -jnp.inf))
    factors = factors * scores[..., None] * dt_blocks[:, None, :, :]
    diag_out = jnp.einsum("cijh,cjhp->cihp", factors, x_blocks, precision=HIGHEST)
    group_end = cumulative[:, -1:, :]
    to_end = jnp.exp(group_end - cumulative) * dt_blocks
    group_states = jnp.einsum("cjh,cjhp,cjn->chpn", to_end, x_blocks, b_blocks, precision=HIGHEST)
    group_decay = jnp.exp(group_end[:, 0, :])
    link_float = link_row.astype(jnp.float32)
    carried = jnp.zeros((head_count, head_size, state_size), jnp.float32)
    entering = [carried]
    carried = link_float[1] * (group_decay[0][:, None, None] * carried + group_states[0])
    entering.append(carried)
    entering = jnp.stack(entering)
    off_out = jnp.einsum(
        "cih,cin,chpn->cihp", jnp.exp(cumulative), c_blocks, entering, precision=HIGHEST
    )
    return (diag_out + off_out).reshape(rows_all, head_count, head_size)


def mixer_slot(
    projected, conv_weight, conv_bias, dt_bias, a_log, skip_gain, gate_gain, fill_row, link_row
):
    rows_all = projected.shape[0]
    groups = fill_row.shape[0]
    length = rows_all // groups
    inner_size = gate_gain.shape[0]
    head_count = dt_bias.shape[0]
    conv_size = conv_bias.shape[0]
    state_size = (conv_size - inner_size) // 2
    head_size = inner_size // head_count
    gate_part = projected[:, :inner_size]
    conv_in = projected[:, inner_size : inner_size + conv_size]
    dt_raw = projected[:, inner_size + conv_size :]
    within = jnp.arange(rows_all) % length
    linked = jnp.broadcast_to(link_row.astype(jnp.float32)[:, None], (groups, length)).reshape(
        rows_all
    )
    filled = jnp.broadcast_to(fill_row[:, None], (groups, length)).reshape(rows_all)
    valid = (within < filled).astype(jnp.float32)
    conv_sum = conv_bias + conv_weight[0] * conv_in
    for lag_steps in range(1, conv_weight.shape[0]):
        shifted = jnp.concatenate(
            [jnp.zeros((lag_steps, conv_size), jnp.float32), conv_in[:-lag_steps]], axis=0
        )
        keep_mask = jnp.maximum((within >= lag_steps).astype(jnp.float32), linked)
        conv_sum = conv_sum + conv_weight[lag_steps] * shifted * keep_mask[:, None]
    activated = jax.nn.silu(conv_sum)
    x_heads = activated[:, :inner_size].reshape(rows_all, head_count, head_size)
    input_b = activated[:, inner_size : inner_size + state_size]
    input_c = activated[:, inner_size + state_size :]
    step_size = jax.nn.softplus(dt_raw + dt_bias)
    log_decay = step_size * -jnp.exp(a_log)
    scanned = ssd_scan(x_heads, step_size, log_decay, input_b, input_c, link_row, groups)
    scanned = scanned + skip_gain[:, None] * x_heads
    gated = scanned.reshape(rows_all, inner_size) * jax.nn.silu(gate_part)
    return norm_map(gated, gate_gain) * valid[:, None]


def outer_term(left_rows, right_rows):
    return lax.dot_general(
        left_rows, right_rows, (((0,), (0,)), ((), ())), preferred_element_type=jnp.float32
    )


def on_device(
    tokens_in,
    out_cotangent,
    in_weight,
    out_weight,
    norm_gain,
    conv_weight,
    conv_bias,
    dt_bias,
    a_log,
    skip_gain,
    gate_gain,
    group_fill,
    group_link,
):
    contract_cols = (((1,), (1,)), ((), ()))
    micro_count = tokens_in.shape[0]
    section_count = lax.axis_size("section")
    section_index = lax.axis_index("section")
    is_first = section_index == 0
    is_last = section_index == section_count - 1
    tick_count = micro_count + section_count - 1
    params = (conv_weight[0], conv_bias[0], dt_bias[0], a_log[0], skip_gain[0], gate_gain[0])
    gain_row = norm_gain[0]
    full_in, full_out = (
        lax.all_gather(in_weight, "dp", axis=1, tiled=True),
        lax.all_gather(out_weight, "dp", axis=1, tiled=True),
    )
    weight_in = full_in[0]
    weight_out = full_out[0]
    tick_list = jnp.arange(tick_count, dtype=jnp.int32)

    def forward_tick(received, tick_index):
        batch_index = jnp.clip(tick_index - section_index, 0, micro_count - 1)
        own_rows = lax.dynamic_index_in_dim(
            tokens_in, jnp.minimum(tick_index, micro_count - 1), 0, keepdims=False
        )
        layer_in = jnp.where(is_first, own_rows, received)
        fill_row = lax.dynamic_index_in_dim(group_fill, batch_index, 0, keepdims=False)
        link_row = lax.dynamic_index_in_dim(group_link, batch_index, 0, keepdims=False)
        residual = layer_in.astype(jnp.float32)
        normed = norm_map(residual, gain_row).astype(jnp.bfloat16)
        projected = jnp.dot(normed, weight_in, preferred_element_type=jnp.float32)
        mixed = mixer_slot(projected, *params, fill_row, link_row).astype(jnp.bfloat16)
        output = residual + jnp.dot(mixed, weight_out, preferred_element_type=jnp.float32)
        sent = shifted_2(output.astype(jnp.bfloat16), "section", 1)
        return (sent, (layer_in, normed, projected, mixed, output))

    start_rows = jnp.zeros(tokens_in.shape[1:], jnp.bfloat16)
    unused_rows, kept = lax.scan(forward_tick, start_rows, tick_list)
    stack_inputs, stack_normed, stack_projected, stack_mixed, stack_outputs = kept
    section_outputs = lax.dynamic_slice_in_dim(stack_outputs, section_index, micro_count, 0)[None]
    again_in, again_out = (
        lax.all_gather(in_weight, "dp", axis=1, tiled=True),
        lax.all_gather(out_weight, "dp", axis=1, tiled=True),
    )
    weight_in = again_in[0]
    weight_out = again_out[0]

    def backward_tick(carry, tick_index):
        back_received, small_sums, shard_in, shard_out = carry
        saved_index = jnp.clip(
            tick_index - section_count + 1 + 2 * section_index, 0, tick_count - 1
        )
        batch_index = jnp.clip(tick_index - section_count + 1 + section_index, 0, micro_count - 1)
        own_grad = lax.dynamic_index_in_dim(
            out_cotangent, jnp.minimum(tick_index, micro_count - 1), 0, keepdims=False
        ).astype(jnp.float32)
        own_grad = jnp.where(tick_index < micro_count, own_grad, jnp.zeros_like(own_grad))
        upstream = jnp.where(is_last, own_grad, back_received.astype(jnp.float32))
        fill_row = lax.dynamic_index_in_dim(group_fill, batch_index, 0, keepdims=False)
        link_row = lax.dynamic_index_in_dim(group_link, batch_index, 0, keepdims=False)
        residual = lax.dynamic_index_in_dim(stack_inputs, saved_index, 0, keepdims=False).astype(
            jnp.float32
        )
        normed = lax.dynamic_index_in_dim(stack_normed, saved_index, 0, keepdims=False)
        projected = lax.dynamic_index_in_dim(stack_projected, saved_index, 0, keepdims=False)
        mixed = lax.dynamic_index_in_dim(stack_mixed, saved_index, 0, keepdims=False)
        upper_lower = upstream.astype(jnp.bfloat16)
        d_mixed = lax.dot_general(
            upper_lower, weight_out, contract_cols, preferred_element_type=jnp.float32
        )

        def local_map(proj_rows, *param_list):
            return mixer_slot(proj_rows, *param_list, fill_row, link_row)

        unused, pull_back = jax.vjp(local_map, projected, *params)
        pulled = pull_back(d_mixed)
        d_low = pulled[0].astype(jnp.bfloat16)
        d_normed = lax.dot_general(
            d_low, weight_in, contract_cols, preferred_element_type=jnp.float32
        )
        unused_norm, pull_norm = jax.vjp(norm_map, residual, gain_row)
        d_residual, d_gain = pull_norm(d_normed)
        input_grad = upstream + d_residual
        tick_small = (d_gain,) + tuple(pulled[1:])
        small_sums = jax.tree.map(jnp.add, small_sums, tick_small)
        sent_back = shifted_2(input_grad.astype(jnp.bfloat16), "section", -1)
        return (
            (sent_back, small_sums, shard_in, shard_out),
            (normed, d_low, mixed, upper_lower, input_grad),
        )

    small_start = jax.tree.map(
        lambda item: jnp.zeros(item.shape, jnp.float32), (gain_row,) + params
    )
    shard_start_in = jnp.zeros(in_weight.shape[1:], jnp.float32)
    shard_start_out = jnp.zeros(out_weight.shape[1:], jnp.float32)
    carry_start = (start_rows, small_start, shard_start_in, shard_start_out)
    carry_end, tick_outputs = lax.scan(backward_tick, carry_start, tick_list)
    unused_back, small_sums, shard_in, shard_out = carry_end
    list_normed, list_dproj, list_mixed, list_uplow, list_grads = tick_outputs
    all_normed = list_normed.reshape(-1, list_normed.shape[-1])
    all_dproj = list_dproj.reshape(-1, list_dproj.shape[-1])
    all_mixed = list_mixed.reshape(-1, list_mixed.shape[-1])
    all_uplow = list_uplow.reshape(-1, list_uplow.shape[-1])
    shard_in = lax.psum_scatter(
        outer_term(all_normed, all_dproj), "dp", scatter_dimension=0, tiled=True
    )
    shard_out = lax.psum_scatter(
        outer_term(all_mixed, all_uplow), "dp", scatter_dimension=0, tiled=True
    )
    summed = lax.psum(small_sums, "dp")
    section_input_grads = lax.dynamic_slice_in_dim(
        list_grads, section_count - 1 - section_index, micro_count, 0
    )[None]
    return (section_outputs, section_input_grads, shard_in[None], shard_out[None]) + tuple(
        (summed_grad[None] for summed_grad in summed)
    )


def solution(mesh):
    in_specs = (
        P(None, "dp", None),
        P(None, "dp", None),
        P("section", "dp", None),
        P("section", "dp", None),
        P("section", None),
        P("section", None, None),
        P("section", None),
        P("section", None),
        P("section", None),
        P("section", None),
        P("section", None),
        P(None, "dp"),
        P(None, "dp"),
    )
    out_specs = (
        P("section", None, "dp", None),
        P("section", None, "dp", None),
        P("section", "dp", None),
        P("section", "dp", None),
        P("section", None),
        P("section", None, None),
        P("section", None),
        P("section", None),
        P("section", None),
        P("section", None),
        P("section", None),
    )
    return jax.shard_map(
        on_device, mesh=mesh, in_specs=in_specs, out_specs=out_specs, check_vma=False
    )
```

profile of v0, /device:TPU:0, one launch (start us, length us, event | category | flops | bytes accessed | tf_op | source)
XLA Modules:
  0.0 1077.1 jit_solution(11850100364788017831)
XLA Ops:
  12.7 50.6 %all-gather.5.cloned.1.call-done = bf16[1,2048,1024]{2,1,0:T(8,128)(2,1)} async-done(((bf16[1,128,1024]{2,1,0:T(8,128)(2,1)}), bf16[1,2048,1024]{2,1,0:T(8,128)(2,1)}) %all-gather.5.cloned.1.call-update) | async-done | bytes 4194320 | tf_op jit(solution)/shard_map/all_gather | solution.py:124
  63.3 80.1 %all-gather.3.cloned.1.call-done = bf16[1,1024,4384]{2,1,0:T(8,128)(2,1)} async-done(((bf16[1,64,4384]{2,1,0:T(8,128)(2,1)}), bf16[1,1024,4384]{2,1,0:T(8,128)(2,1)}) %all-gather.3.cloned.1.call-update) | async-done | bytes 8978448 | tf_op jit(solution)/shard_map/all_gather | solution.py:123
  147.9 184.0 %while.61 = (s32[]{:T(128)}, bf16[64,1024]{1,0:T(8,128)(2,1)S(1)}, bf16[4,64,1024]{2,1,0:T(8,128)(2,1)}, bf16[4,64,1024]{2,1,0:T(8,128)(2,1)}, f32[4,64,4384]{2,...) while((s32[]{:T(128)}, bf16[64,1024]{1,0:T(8,128)(2,1)S(1)}, ...), condition=%wide.region_4.5_spmd, body=%wide.region_0.4_spmd.sunk | while | flops 1205211648 | bytes 37663164 | solution.py:147
  153.6 6.4 bitcast_dynamic-update-slice_fusion.17
  171.9 2.5 convolution_bitcast_fusion.9
  174.4 2.8 fusion.257
  177.2 3.3 fusion.258
  184.0 3.1 fusion.260
  187.1 3.4 collective-permute-start
  199.3 6.4 bitcast_dynamic-update-slice_fusion.17
  217.6 2.5 convolution_bitcast_fusion.9
  220.2 2.8 fusion.257
  223.0 3.3 fusion.258
  229.7 3.1 fusion.260
  232.8 4.4 collective-permute-start
  245.4 6.4 bitcast_dynamic-update-slice_fusion.17
  263.7 2.5 convolution_bitcast_fusion.9
  266.3 2.8 fusion.257
  269.1 3.3 fusion.258
  275.9 3.1 fusion.260
  279.0 4.4 collective-permute-start
  291.5 6.4 bitcast_dynamic-update-slice_fusion.17
  309.8 2.5 convolution_bitcast_fusion.9
  312.4 2.8 fusion.257
  315.2 3.3 fusion.258
  321.9 3.1 fusion.260
  325.0 4.4 collective-permute-start
  336.5 430.2 %while.62 = (s32[]{:T(128)}, bf16[64,1024]{1,0:T(8,128)(2,1)S(1)}, f32[1024]{0:T(1024)}, f32[4,2304]{1,0:T(4,128)}, f32[2304]{0:T(1024)}, /*index=5*/f32[32]{0:T...) while((s32[]{:T(128)}, bf16[64,1024]{1,0:T(8,128)(2,1)S(1)}, ...), condition=%wide.region_29.30_spmd.clone, body=%wide.region_5.29_spmd.clone.sunk | while | flops 1929479168 | bytes 110034496 | solution.py:207
  376.7 3.5 fusion.292
  392.4 4.4 multiply_reduce_fusion.25
  405.0 4.1 fusion.300
  409.2 3.9 multiply_reduce_fusion.27
  413.1 2.5 fusion.299
  415.6 3.2 fusion.297
  420.2 3.7 fusion.298
  444.0 6.7 fusion.305
  479.1 3.5 fusion.292
  494.8 4.4 multiply_reduce_fusion.25
  507.3 4.1 fusion.300
  511.5 3.9 multiply_reduce_fusion.27
  515.4 2.5 fusion.299
  517.9 3.2 fusion.297
  522.6 3.7 fusion.298
  546.3 6.7 fusion.305
  581.4 3.5 fusion.292
  597.1 4.4 multiply_reduce_fusion.25
  609.7 4.1 fusion.300
  613.8 3.9 multiply_reduce_fusion.27
  617.7 2.5 fusion.299
  620.2 3.2 fusion.297
  624.9 3.7 fusion.298
  648.6 6.7 fusion.305
  683.8 3.5 fusion.292
  699.5 4.4 multiply_reduce_fusion.25
  712.0 4.1 fusion.300
  716.2 3.9 multiply_reduce_fusion.27
  722.6 3.2 fusion.297
  727.3 3.7 fusion.298
  751.0 6.7 fusion.305
  766.7 6.0 convolution_bitcast_fusion.6
  774.5 8.9 convolution_bitcast_fusion.5
  784.3 61.2 %all-reduce.24 = (f32[1,1024]{1,0:T(1,128)}, f32[1,4,2304]{2,1,0:T(4,128)}, f32[1,2304]{1,0:T(1,128)}, f32[1,32]{1,0:T(1,128)}, f32[1,32]{1,0:T(1,128)}, /*index=5*/f32[1,32]{1,0:T(1,128)}, f32[1,2048]{1,0:T(1,128)}) all-reduce(f32[1,1024]{1,0:T(1,128)S(1)} %bitcast.403, ...), channel_id=1, replica_groups=mesh['section'=2,'dp'=16] {'dp'}, use_global_device_ids=true, to_apply=%region_32.33 | all-reduce | flops 14688 | bytes 117504 | tf_op jit(solution)/shard_map/psum | solution.py:220
  846.8 29.4 %reduce-scatter.5.cloned.1.call-done = f32[128,1024]{1,0:T(8,128)} async-done(((f32[2048,1024]{1,0:T(8,128)}), f32[128,1024]{1,0:T(8,128)}) %reduce-scatter.5.cloned.1.call-update) | async-done | bytes 524304 | tf_op jit(solution)/shard_map/reduce_scatter | solution.py:217
  876.1 194.0 %reduce-scatter.3.cloned.1.call-done = f32[64,4384]{1,0:T(8,128)} async-done(((f32[1024,4384]{1,0:T(8,128)}), f32[64,4384]{1,0:T(8,128)}) %reduce-scatter.3.cloned.1.call-update) | async-done | bytes 1122320 | tf_op jit(solution)/shard_map/reduce_scatter | solution.py:214
  (1325 shorter events, 378.9 us)
Async XLA Ops:
  7.2 140.7 %copy-start.28 = (f32[1,2048]{1,0:T(1,128)S(1)}, f32[1,2048]{1,0:T(1,128)}, u32[]{:S(2)}) copy-start(f32[1,2048]{1,0:T(1,128)} %param.27) | copy-start | bytes 24580
  7.2 140.7 %copy-start.27 = (f32[1,1024]{1,0:T(1,128)S(1)}, f32[1,1024]{1,0:T(1,128)}, u32[]{:S(2)}) copy-start(f32[1,1024]{1,0:T(1,128)} %param.21) | copy-start | bytes 12292
  7.2 56.1 %all-gather.5.cloned.1.call-start = ((), (), s32[]{:S(2)}) async-start(), calls=%async_computation.3 | async-start | bytes 4456448 | tf_op jit(solution)/shard_map/all_gather | solution.py:124
  7.9 135.4 %all-gather.3.cloned.1.call-start = ((), (), s32[]{:S(2)}) async-start(), calls=%async_computation.2 | async-start | bytes 9748480 | tf_op jit(solution)/shard_map/all_gather | solution.py:123
  8.7 867.4 %reduce-scatter.5.cloned.1.call-start = ((), (), s32[]{:S(2)}) async-start(), calls=%async_computation.5 | async-start | bytes 8912896 | tf_op jit(solution)/shard_map/reduce_scatter | solution.py:217
  184.0 8.0 copy-start.78
  187.1 6.5 collective-permute-start
  229.7 9.1 copy-start.78
  232.8 6.9 collective-permute-start
  275.9 9.0 copy-start.78
  279.0 6.9 collective-permute-start
  321.9 9.0 copy-start.78
  325.0 6.9 collective-permute-start
  357.2 35.3 %copy-start.12 = (bf16[64,1024]{1,0:T(8,128)(2,1)}, bf16[64,1024]{1,0:T(8,128)(2,1)S(1)}, u32[]{:S(2)}) copy-start(bf16[64,1024]{1,0:T(8,128)(2,1)S(1)} %get-tuple-element.2087) | copy-start | bytes 393220 | tf_op jit(solution)/shard_map/while
  405.0 8.1 copy-start.19
  420.2 8.8 copy-start.35
  423.9 9.0 copy-start.8
  423.9 9.0 copy-start.30
  425.0 9.0 copy-start.97
  443.9 9.9 copy-start.60
  443.9 10.1 copy-start.54
  443.9 10.1 copy-start.56
  443.9 10.1 copy-start.55
  444.0 10.2 copy-start.58
  452.5 6.8 collective-permute-start.1
  459.5 35.3 %copy-start.12 = (bf16[64,1024]{1,0:T(8,128)(2,1)}, bf16[64,1024]{1,0:T(8,128)(2,1)S(1)}, u32[]{:S(2)}) copy-start(bf16[64,1024]{1,0:T(8,128)(2,1)S(1)} %get-tuple-element.2087) | copy-start | bytes 393220 | tf_op jit(solution)/shard_map/while
  507.3 8.1 copy-start.19
  522.6 8.8 copy-start.35
  526.2 9.0 copy-start.8
  526.2 9.0 copy-start.30
  527.3 9.0 copy-start.97
  546.2 9.9 copy-start.60
  546.2 10.1 copy-start.54
  546.3 10.1 copy-start.56
  546.3 10.2 copy-start.55
  546.3 10.2 copy-start.58
  554.9 6.8 collective-permute-start.1
  561.8 35.3 %copy-start.12 = (bf16[64,1024]{1,0:T(8,128)(2,1)}, bf16[64,1024]{1,0:T(8,128)(2,1)S(1)}, u32[]{:S(2)}) copy-start(bf16[64,1024]{1,0:T(8,128)(2,1)S(1)} %get-tuple-element.2087) | copy-start | bytes 393220 | tf_op jit(solution)/shard_map/while
  609.7 8.1 copy-start.19
  624.9 8.8 copy-start.35
  628.6 9.0 copy-start.8
  628.6 9.0 copy-start.30
  629.7 9.0 copy-start.97
  648.6 9.9 copy-start.60
  648.6 10.1 copy-start.54
  648.6 10.1 copy-start.56
  648.6 10.2 copy-start.55
  648.6 10.2 copy-start.58
  657.2 6.8 collective-permute-start.1
  664.2 35.3 %copy-start.12 = (bf16[64,1024]{1,0:T(8,128)(2,1)}, bf16[64,1024]{1,0:T(8,128)(2,1)S(1)}, u32[]{:S(2)}) copy-start(bf16[64,1024]{1,0:T(8,128)(2,1)S(1)} %get-tuple-element.2087) | copy-start | bytes 393220 | tf_op jit(solution)/shard_map/while
  712.0 8.1 copy-start.19
  727.2 8.8 copy-start.35
  730.9 9.0 copy-start.8
  730.9 9.0 copy-start.30
  732.0 9.0 copy-start.97
  750.9 9.9 copy-start.60
  750.9 10.1 copy-start.54
  750.9 10.1 copy-start.56
  751.0 10.1 copy-start.55
  751.0 10.2 copy-start.58
  759.6 6.8 collective-permute-start.1
  772.7 297.4 %reduce-scatter.3.cloned.1.call-start = ((), (), s32[]{:S(2)}) async-start(), calls=%async_computation.4 | async-start | bytes 19496960 | tf_op jit(solution)/shard_map/reduce_scatter | solution.py:214
  783.5 62.0 %copy-start.43 = (f32[4,64,1024]{2,1,0:T(8,128)S(1)}, f32[4,64,1024]{2,1,0:T(8,128)}, u32[]{:S(2)}) copy-start(f32[4,64,1024]{2,1,0:T(8,128)} %get-tuple-element.969) | copy-start | bytes 3145732
  783.5 62.0 %copy-start.44 = (f32[4,64,1024]{2,1,0:T(8,128)S(1)}, f32[4,64,1024]{2,1,0:T(8,128)}, u32[]{:S(2)}) copy-start(f32[4,64,1024]{2,1,0:T(8,128)} %get-tuple-element.964) | copy-start | bytes 3145732
  (325 other events, 1400.6 us)
Sparse Core Ops, SparseCore 0:
  10.2 53.0 all-gather.4
  65.6 77.7 all-gather.2
  772.9 103.2 reduce-scatter.4
  880.8 189.3 reduce-scatter.2
where the time goes:
time: 1090 us; the launch traced here: 1080 us
  waiting for transfers between devices  360 us (33%)
  matrix products  249 us (23%)
  local copies, waits for them, and re-layouts  170 us (16%)
  other arithmetic  161 us (15%)
  blocking collectives  61.2 us (6%)
  loops' own time  39.4 us (4%)
  starting transfers between devices  21.8 us (2%)
  between operations  14.3 us (1%)
    reduce_scatter x1, waiting for transfers between devices, on_device(): lax.psum_scatter(outer_term(all_normed, all_dproj), 'dp', scatter_dimensi...  194 us
    all_gather x1, waiting for transfers between devices, on_device(): lax.all_gather(in_weight, 'dp', axis=1, tiled=True)  80.1 us
    psum x1, blocking collectives, on_device(): summed = lax.psum(small_sums, 'dp')  61.2 us
    all_gather x1, waiting for transfers between devices, on_device(): lax.all_gather(out_weight, 'dp', axis=1, tiled=True)  50.6 us
    dot_general x16, matrix products, ssd_scan(): jnp.einsum('cijh,cjhp->cihp', factors, x_blocks, precision=HIGHEST)  48.8 us
    another operation x1, loops' own time, on_device(): carry_end, tick_outputs = lax.scan(backward_tick, carry_start, tick_list)  33.3 us
    dot_general x12, matrix products, ssd_scan(): jnp.einsum('cih,cin,chpn->cihp', jnp.exp(cumulative), c_blocks, entering,...  31.7 us
    reduce_scatter x1, waiting for transfers between devices, on_device(): lax.psum_scatter(outer_term(all_mixed, all_uplow), 'dp', scatter_dimensio...  29.4 us
  transfers between devices with their start and end apart: 12, of which 12 were waited for; matrix products, arithmetic and copies ran while one was open for 4% of the time, Pallas kernels for 0%

commit v1 on v0

--- a/solution.py
+++ b/solution.py
@@ -119,8 +119,23 @@
     tick_count = micro_count + section_count - 1
     params = (conv_weight[0], conv_bias[0], dt_bias[0], a_log[0], skip_gain[0], gate_gain[0])
     gain_row = norm_gain[0]
+
+    def _place_files(xin):
+        num_devices = lax.axis_size("dp")
+        in_order = list(map(lambda m: (m, (m + 1) % num_devices), range(num_devices)))
+        entries = list(map(lambda m: (m, (m - 1) % num_devices), range(num_devices)))
+        r2, now = ([xin], [xin])
+        for _ in range(num_devices // 2):
+            r2.append(lax.ppermute(r2[-1], "dp", in_order))
+        for _ in [*range((num_devices - 1) // 2)]:
+            now.append(lax.ppermute(now[-1], "dp", entries))
+        val2 = jnp.concatenate([*r2[::-1], *now[1:]], axis=1)
+        return jnp.roll(
+            val2, shift=(lax.axis_index("dp") - num_devices // 2) * xin.shape[1], axis=1
+        )
+
     full_in, full_out = (
-        lax.all_gather(in_weight, "dp", axis=1, tiled=True),
+        _place_files(in_weight),
         lax.all_gather(out_weight, "dp", axis=1, tiled=True),
     )
     weight_in = full_in[0]

time: 1090 us -> 1250 us (1.15)
  local copies, waits for them, and re-layouts: 170 us -> 254 us
  waiting for transfers between devices: 360 us -> 312 us
  other arithmetic: 161 us -> 207 us
  starting transfers between devices: 21.8 us -> 56.3 us
  matrix products: 249 us -> 279 us
    all_gather x1, waiting for transfers between devices: 80.1 us -> 0.01 us  [on_device(): lax.all_gather(in_weight, 'dp', axis=1, tiled=True)]
    ppermute x0 -> x15, waiting for transfers between devices: none -> 79 us  [the longest x8 76.9 us: _place_files(): r2.append(lax.ppermute(r2[-1], 'dp', in_order))]
    all_gather x1, waiting for transfers between devices: 50.6 us -> 0.01 us  [on_device(): lax.all_gather(out_weight, 'dp', axis=1, tiled=True)]
    unnamed x26 -> x77, local copies, waits for them, and re-layouts: 2.49 us -> 43.3 us
    ppermute x0 -> x15, starting transfers between devices: none -> 34.1 us  [the longest x7 32.7 us: _place_files(): now.append(lax.ppermute(now[-1], 'dp', entries))]
    add x24, other arithmetic: 0.44 us -> 23.8 us  [backward_tick(): small_sums = jax.tree.map(jnp.add, small_sums, tick_small)]
  transfers between devices with their start and end apart: 12 -> 27, of which waited for: 12 -> 16; matrix products, arithmetic and copies ran while one was open for 4% -> 23% of each run, Pallas kernels for 0% -> 0%
where the time goes in v1:
time: 1250 us; the launch traced here: 1230 us
  waiting for transfers between devices  312 us (25%)
  matrix products  279 us (22%)
  local copies, waits for them, and re-layouts  254 us (20%)
  other arithmetic  207 us (17%)
  blocking collectives  73.1 us (6%)
  starting transfers between devices  56.3 us (5%)
  loops' own time  36.6 us (3%)
  between operations  14.5 us (1%)
    reduce_scatter x1, waiting for transfers between devices, on_device(): lax.psum_scatter(outer_term(all_normed, all_dproj), 'dp', scatter_dimensi...  194 us
    ppermute x8, waiting for transfers between devices, _place_files(): r2.append(lax.ppermute(r2[-1], 'dp', in_order))  76.9 us
    psum x1, blocking collectives, on_device(): summed = lax.psum(small_sums, 'dp')  73.1 us
    dot_general x16, matrix products, ssd_scan(): jnp.einsum('cijh,cjhp->cihp', factors, x_blocks, precision=HIGHEST)  54.8 us
    unnamed x77, local copies, waits for them, and re-layouts  43.3 us
    dot_general x12, matrix products, ssd_scan(): jnp.einsum('cih,cin,chpn->cihp', jnp.exp(cumulative), c_blocks, entering,...  39.6 us
    reduce_scatter x1, waiting for transfers between devices, on_device(): lax.psum_scatter(outer_term(all_mixed, all_uplow), 'dp', scatter_dimensio...  37.7 us
    ppermute x7, starting transfers between devices, _place_files(): now.append(lax.ppermute(now[-1], 'dp', entries))  32.7 us
  transfers between devices with their start and end apart: 27, of which 16 were waited for; matrix products, arithmetic and copies ran while one was open for 23% of the time, Pallas kernels for 0%

profile of v1, /device:TPU:0, one launch (start us, length us, event | category | flops | bytes accessed | tf_op | source)
XLA Modules:
  0.0 1232.8 jit_solution(1844961109799457680)
XLA Ops:
  8.5 12.6 %collective-permute-done.2 = bf16[1,64,4384]{2,1,0:T(8,128)(2,1)S(1)} collective-permute-done((bf16[1,64,4384]{2,1,0:T(8,128)(2,1)}, bf16[1,64,4384]{2,1,0:T(8,128)(2,1)S(1)}, u32[]{:S(2)}, u32[]{:S(2)}) %collective-permute-start.2) | collective-permute-done | bytes 561184 | tf_op jit(solution)/shard_map/ppermute | solution.py:129
  21.1 4.4 collective-permute-start.10
  25.5 15.5 %collective-permute-done.3 = bf16[1,64,4384]{2,1,0:T(8,128)(2,1)S(1)} collective-permute-done((bf16[1,64,4384]{2,1,0:T(8,128)(2,1)S(1)}, bf16[1,64,4384]{2,1,0:T(8,128)(2,1)S(1)}, u32[]{:S(2)}, u32[]{:S(2)}) %collective-permute-start.3) | collective-permute-done | bytes 561184 | tf_op jit(solution)/shard_map/ppermute | solution.py:129
  41.0 4.4 collective-permute-start.11
  45.5 12.8 %collective-permute-done.4 = bf16[1,64,4384]{2,1,0:T(8,128)(2,1)S(1)} collective-permute-done((bf16[1,64,4384]{2,1,0:T(8,128)(2,1)S(1)}, bf16[1,64,4384]{2,1,0:T(8,128)(2,1)S(1)}, u32[]{:S(2)}, u32[]{:S(2)}) %collective-permute-start.4) | collective-permute-done | bytes 561184 | tf_op jit(solution)/shard_map/ppermute | solution.py:129
  59.8 4.6 collective-permute-start.12
  64.4 7.9 collective-permute-done.5
  74.0 4.5 collective-permute-start.13
  78.5 11.4 collective-permute-done.6
  90.8 4.4 collective-permute-start.14
  95.1 6.7 collective-permute-done.7
  102.4 4.8 collective-permute-start.15
  107.2 6.7 collective-permute-done.8
  118.2 5.5 collective-permute-start.16
  123.7 3.5 collective-permute-done.9
  169.6 7.8 dynamic-slice_bitcast_fusion.1
  182.0 189.3 %while.61 = (s32[]{:T(128)}, bf16[64,1024]{1,0:T(8,128)(2,1)S(1)}, bf16[4,64,1024]{2,1,0:T(8,128)(2,1)}, bf16[4,64,1024]{2,1,0:T(8,128)(2,1)}, f32[4,64,4384]{2,...) while((s32[]{:T(128)}, bf16[64,1024]{1,0:T(8,128)(2,1)S(1)}, ...), condition=%wide.region_4.5_spmd, body=%wide.region_0.4_spmd.sunk | while | flops 1205211648 | bytes 37600076 | solution.py:162
  185.8 6.4 bitcast_dynamic-update-slice_fusion.17
  205.3 3.5 fusion.257
  222.8 3.8 collective-permute-start
  232.7 6.4 bitcast_dynamic-update-slice_fusion.17
  269.7 4.4 collective-permute-start
  280.1 6.4 bitcast_dynamic-update-slice_fusion.17
  317.0 4.4 collective-permute-start
  327.5 6.4 bitcast_dynamic-update-slice_fusion.17
  364.5 4.4 collective-permute-start
  375.9 528.0 %while.62 = (s32[]{:T(128)}, bf16[64,1024]{1,0:T(8,128)(2,1)S(1)}, f32[1024]{0:T(1024)}, f32[4,2304]{1,0:T(4,128)}, f32[2304]{0:T(1024)}, /*index=5*/f32[32]{0:T...) while((s32[]{:T(128)}, bf16[64,1024]{1,0:T(8,128)(2,1)S(1)}, ...), condition=%wide.region_29.30_spmd.clone, body=%wide.region_5.29_spmd.clone.sunk | while | flops 1929479168 | bytes 86325424 | solution.py:222
  420.3 3.5 fusion.292
  445.7 4.4 multiply_reduce_fusion.25
  455.3 4.5 multiply_reduce_fusion.27
  459.8 5.0 fusion.300
  467.4 3.6 fusion.301
  471.0 4.0 fusion.297
  479.6 3.5 fusion.298
  501.1 6.8 fusion.305
  545.5 3.5 fusion.292
  570.9 4.4 multiply_reduce_fusion.25
  580.6 4.5 multiply_reduce_fusion.27
  585.0 5.0 fusion.300
  592.6 3.6 fusion.301
  596.2 4.0 fusion.297
  604.9 3.5 fusion.298
  626.3 6.8 fusion.305
  672.9 3.5 fusion.292
  698.3 4.4 multiply_reduce_fusion.25
  708.0 4.5 multiply_reduce_fusion.27
  712.4 5.0 fusion.300
  720.0 3.6 fusion.301
  723.6 4.0 fusion.297
  732.3 3.5 fusion.298
  753.7 6.8 fusion.305
  800.2 3.5 fusion.292
  825.6 4.4 multiply_reduce_fusion.25
  835.3 4.5 multiply_reduce_fusion.27
  839.8 5.0 fusion.300
  847.3 3.6 fusion.301
  851.0 4.0 fusion.297
  859.6 3.5 fusion.298
  881.0 6.8 fusion.305
  903.9 6.0 convolution_bitcast_fusion.6
  910.2 9.5 convolution_bitcast_fusion.5
  919.8 73.1 %all-reduce.24 = (f32[1,1024]{1,0:T(1,128)}, f32[1,4,2304]{2,1,0:T(4,128)}, f32[1,2304]{1,0:T(1,128)}, f32[1,32]{1,0:T(1,128)}, f32[1,32]{1,0:T(1,128)}, /*index=5*/f32[1,32]{1,0:T(1,128)}, f32[1,2048]{1,0:T(1,128)}) all-reduce(f32[1,1024]{1,0:T(1,128)S(1)} %bitcast.405, ...), channel_id=1, replica_groups=mesh['section'=2,'dp'=16] {'dp'}, use_global_device_ids=true, to_apply=%region_32.33 | all-reduce | flops 14688 | bytes 117504 | tf_op jit(solution)/shard_map/psum | solution.py:235
  994.2 37.7 %reduce-scatter.5.cloned.1.call-done = f32[128,1024]{1,0:T(8,128)} async-done(((f32[2048,1024]{1,0:T(8,128)}), f32[128,1024]{1,0:T(8,128)}) %reduce-scatter.5.cloned.1.call-update) | async-done | bytes 524304 | tf_op jit(solution)/shard_map/reduce_scatter | solution.py:232
  1031.8 194.0 %reduce-scatter.3.cloned.1.call-done = f32[64,4384]{1,0:T(8,128)} async-done(((f32[1024,4384]{1,0:T(8,128)}), f32[64,4384]{1,0:T(8,128)}) %reduce-scatter.3.cloned.1.call-update) | async-done | bytes 1122320 | tf_op jit(solution)/shard_map/reduce_scatter | solution.py:229
  (872 shorter events, 557.0 us)
Async XLA Ops:
  7.2 153.4 %copy-start.10 = (bf16[1,64,4384]{2,1,0:T(8,128)(2,1)S(1)}, bf16[1,64,4384]{2,1,0:T(8,128)(2,1)}, u32[]{:S(2)}) copy-start(bf16[1,64,4384]{2,1,0:T(8,128)(2,1)} %param.19) | copy-start | bytes 1683460
  7.2 170.3 %all-gather.3.cloned.1.call-start = ((), (), s32[]{:S(2)}) async-start(), calls=%async_computation.2 | async-start | bytes 4456448 | tf_op jit(solution)/shard_map/all_gather | solution.py:139
  7.9 363.4 %all-gather.5.cloned.1.call-start = ((), (), s32[]{:S(2)}) async-start(), calls=%async_computation.3 | async-start | bytes 9748480 | tf_op jit(solution)/shard_map/all_gather | solution.py:166
  8.0 13.1 %collective-permute-start.2 = (bf16[1,64,4384]{2,1,0:T(8,128)(2,1)}, bf16[1,64,4384]{2,1,0:T(8,128)(2,1)S(1)}, u32[]{:S(2)}, u32[]{:S(2)}) collective-permute-start(bf16[1,64,4384]{2,1,0:T(8,128)(2,1)} %param.19), channel_id=1, source_target_pairs={{0,1},{1,2},{2,3},{3,4},{4,5},{5,6},{6,7},{7,8},{8,9},{9,10},{10,1... | collective-permute-start | bytes 1683464 | tf_op jit(solution)/shard_map/ppermute | solution.py:129
  21.1 19.9 %collective-permute-start.3 = (bf16[1,64,4384]{2,1,0:T(8,128)(2,1)S(1)}, bf16[1,64,4384]{2,1,0:T(8,128)(2,1)S(1)}, u32[]{:S(2)}, u32[]{:S(2)}) collective-permute-start(bf16[1,64,4384]{2,1,0:T(8,128)(2,1)S(1)} %collective-permute-done.2), channel_id=1, source_target_pairs={{0,1},{1,2},{2,3},{3,4},{4,5},{5,6},{6,7},{7,8},{8,9},{9,10},{10,1... | collective-permute-start | bytes 1683464 | tf_op jit(solution)/shard_map/ppermute | solution.py:129
  21.1 19.9 %collective-permute-start.10 = (bf16[1,64,4384]{2,1,0:T(8,128)(2,1)}, bf16[1,64,4384]{2,1,0:T(8,128)(2,1)S(1)}, u32[]{:S(2)}, u32[]{:S(2)}) collective-permute-start(bf16[1,64,4384]{2,1,0:T(8,128)(2,1)} %param.19), channel_id=1, source_target_pairs={{0,15},{1,0},{2,1},{3,2},{4,3},{5,4},{6,5},{7,6},{8,7},{9,8},{10,9... | collective-permute-start | bytes 1683464 | tf_op jit(solution)/shard_map/ppermute | solution.py:131
  41.0 17.3 %collective-permute-start.4 = (bf16[1,64,4384]{2,1,0:T(8,128)(2,1)S(1)}, bf16[1,64,4384]{2,1,0:T(8,128)(2,1)S(1)}, u32[]{:S(2)}, u32[]{:S(2)}) collective-permute-start(bf16[1,64,4384]{2,1,0:T(8,128)(2,1)S(1)} %collective-permute-done.3), channel_id=1, source_target_pairs={{0,1},{1,2},{2,3},{3,4},{4,5},{5,6},{6,7},{7,8},{8,9},{9,10},{10,1... | collective-permute-start | bytes 1683464 | tf_op jit(solution)/shard_map/ppermute | solution.py:129
  41.0 18.8 %collective-permute-start.11 = (bf16[1,64,4384]{2,1,0:T(8,128)(2,1)S(1)}, bf16[1,64,4384]{2,1,0:T(8,128)(2,1)S(1)}, u32[]{:S(2)}, u32[]{:S(2)}) collective-permute-start(bf16[1,64,4384]{2,1,0:T(8,128)(2,1)S(1)} %collective-permute-done.10), channel_id=1, source_target_pairs={{0,15},{1,0},{2,1},{3,2},{4,3},{5,4},{6,5},{7,6},{8,7},{9,8},{10,9... | collective-permute-start | bytes 1683464 | tf_op jit(solution)/shard_map/ppermute | solution.py:131
  58.3 14.0 %collective-permute-start.5 = (bf16[1,64,4384]{2,1,0:T(8,128)(2,1)S(1)}, bf16[1,64,4384]{2,1,0:T(8,128)(2,1)S(1)}, u32[]{:S(2)}, u32[]{:S(2)}) collective-permute-start(bf16[1,64,4384]{2,1,0:T(8,128)(2,1)S(1)} %collective-permute-done.4), channel_id=1, source_target_pairs={{0,1},{1,2},{2,3},{3,4},{4,5},{5,6},{6,7},{7,8},{8,9},{9,10},{10,1... | collective-permute-start | bytes 1683464 | tf_op jit(solution)/shard_map/ppermute | solution.py:129
  59.8 13.4 %collective-permute-start.12 = (bf16[1,64,4384]{2,1,0:T(8,128)(2,1)S(1)}, bf16[1,64,4384]{2,1,0:T(8,128)(2,1)S(1)}, u32[]{:S(2)}, u32[]{:S(2)}) collective-permute-start(bf16[1,64,4384]{2,1,0:T(8,128)(2,1)S(1)} %collective-permute-done.11), channel_id=1, source_target_pairs={{0,15},{1,0},{2,1},{3,2},{4,3},{5,4},{6,5},{7,6},{8,7},{9,8},{10,9... | collective-permute-start | bytes 1683464 | tf_op jit(solution)/shard_map/ppermute | solution.py:131
  72.3 30.1 %copy-start.23 = (bf16[1,64,4384]{2,1,0:T(8,128)(2,1)}, bf16[1,64,4384]{2,1,0:T(8,128)(2,1)S(1)}, u32[]{:S(2)}) copy-start(bf16[1,64,4384]{2,1,0:T(8,128)(2,1)S(1)} %collective-permute-done.5) | copy-start | bytes 1683460
  72.3 17.6 %collective-permute-start.6 = (bf16[1,64,4384]{2,1,0:T(8,128)(2,1)S(1)}, bf16[1,64,4384]{2,1,0:T(8,128)(2,1)S(1)}, u32[]{:S(2)}, u32[]{:S(2)}) collective-permute-start(bf16[1,64,4384]{2,1,0:T(8,128)(2,1)S(1)} %collective-permute-done.5), channel_id=1, source_target_pairs={{0,1},{1,2},{2,3},{3,4},{4,5},{5,6},{6,7},{7,8},{8,9},{9,10},{10,1... | collective-permute-start | bytes 1683464 | tf_op jit(solution)/shard_map/ppermute | solution.py:129
  74.0 15.9 %collective-permute-start.13 = (bf16[1,64,4384]{2,1,0:T(8,128)(2,1)S(1)}, bf16[1,64,4384]{2,1,0:T(8,128)(2,1)S(1)}, u32[]{:S(2)}, u32[]{:S(2)}) collective-permute-start(bf16[1,64,4384]{2,1,0:T(8,128)(2,1)S(1)} %collective-permute-done.12), channel_id=1, source_target_pairs={{0,15},{1,0},{2,1},{3,2},{4,3},{5,4},{6,5},{7,6},{8,7},{9,8},{10,9... | collective-permute-start | bytes 1683464 | tf_op jit(solution)/shard_map/ppermute | solution.py:131
  89.9 11.9 collective-permute-start.7
  90.8 11.6 collective-permute-start.14
  101.8 12.0 collective-permute-start.8
  102.4 15.8 %collective-permute-start.15 = (bf16[1,64,4384]{2,1,0:T(8,128)(2,1)}, bf16[1,64,4384]{2,1,0:T(8,128)(2,1)}, u32[]{:S(2)}, u32[]{:S(2)}) collective-permute-start(bf16[1,64,4384]{2,1,0:T(8,128)(2,1)} %collective-permute-done.14), channel_id=1, source_target_pairs={{0,15},{1,0},{2,1},{3,2},{4,3},{5,4},{6,5},{7,6},{8,7},{9,8},{10,9... | collective-permute-start | bytes 1683464 | tf_op jit(solution)/shard_map/ppermute | solution.py:131
  113.9 13.3 %collective-permute-start.9 = (bf16[1,64,4384]{2,1,0:T(8,128)(2,1)}, bf16[1,64,4384]{2,1,0:T(8,128)(2,1)}, u32[]{:S(2)}, u32[]{:S(2)}) collective-permute-start(bf16[1,64,4384]{2,1,0:T(8,128)(2,1)} %collective-permute-done.8), channel_id=1, source_target_pairs={{0,1},{1,2},{2,3},{3,4},{4,5},{5,6},{6,7},{7,8},{8,9},{9,10},{10,1... | collective-permute-start | bytes 1683464 | tf_op jit(solution)/shard_map/ppermute | solution.py:129
  113.9 917.9 %reduce-scatter.5.cloned.1.call-start = ((), (), s32[]{:S(2)}) async-start(), calls=%async_computation.5 | async-start | bytes 8912896 | tf_op jit(solution)/shard_map/reduce_scatter | solution.py:232
  116.7 38.6 %copy-start.28 = (bf16[1,64,4384]{2,1,0:T(8,128)(2,1)S(1)}, bf16[1,64,4384]{2,1,0:T(8,128)(2,1)}, u32[]{:S(2)}) copy-start(bf16[1,64,4384]{2,1,0:T(8,128)(2,1)} %copy-done.27) | copy-start | bytes 1683460
  116.7 39.5 %copy-start.26 = (bf16[1,64,4384]{2,1,0:T(8,128)(2,1)S(1)}, bf16[1,64,4384]{2,1,0:T(8,128)(2,1)}, u32[]{:S(2)}) copy-start(bf16[1,64,4384]{2,1,0:T(8,128)(2,1)} %copy-done.25) | copy-start | bytes 1683460
  116.7 40.4 %copy-start.24 = (bf16[1,64,4384]{2,1,0:T(8,128)(2,1)S(1)}, bf16[1,64,4384]{2,1,0:T(8,128)(2,1)}, u32[]{:S(2)}) copy-start(bf16[1,64,4384]{2,1,0:T(8,128)(2,1)} %copy-done.23) | copy-start | bytes 1683460
  116.7 46.4 %copy-start.20 = (bf16[1,64,4384]{2,1,0:T(8,128)(2,1)S(1)}, bf16[1,64,4384]{2,1,0:T(8,128)(2,1)}, u32[]{:S(2)}) copy-start(bf16[1,64,4384]{2,1,0:T(8,128)(2,1)} %copy-done.19) | copy-start | bytes 1683460
  116.8 47.3 %copy-start.22 = (bf16[1,64,4384]{2,1,0:T(8,128)(2,1)S(1)}, bf16[1,64,4384]{2,1,0:T(8,128)(2,1)}, u32[]{:S(2)}) copy-start(bf16[1,64,4384]{2,1,0:T(8,128)(2,1)} %copy-done.21) | copy-start | bytes 1683460
  118.2 32.5 %collective-permute-start.16 = (bf16[1,64,4384]{2,1,0:T(8,128)(2,1)}, bf16[1,64,4384]{2,1,0:T(8,128)(2,1)S(1)}, u32[]{:S(2)}, u32[]{:S(2)}) collective-permute-start(bf16[1,64,4384]{2,1,0:T(8,128)(2,1)} %collective-permute-done.15), channel_id=1, source_target_pairs={{0,15},{1,0},{2,1},{3,2},{4,3},{5,4},{6,5},{7,6},{8,7},{9,8},{10,9... | collective-permute-start | bytes 1683464 | tf_op jit(solution)/shard_map/ppermute | solution.py:131
  202.4 25.8 %copy-start.39 = (f32[64]{0:T(128)S(1)}, f32[64]{0:T(128)}, u32[]{:S(2)}) copy-start(f32[64]{0:T(128)} %copy-done.38) | copy-start | bytes 772 | tf_op jit(solution)/shard_map/while
  222.8 6.3 collective-permute-start
  249.2 26.4 %copy-start.39 = (f32[64]{0:T(128)S(1)}, f32[64]{0:T(128)}, u32[]{:S(2)}) copy-start(f32[64]{0:T(128)} %copy-done.38) | copy-start | bytes 772 | tf_op jit(solution)/shard_map/while
  269.7 6.9 collective-permute-start
  296.6 26.4 %copy-start.39 = (f32[64]{0:T(128)S(1)}, f32[64]{0:T(128)}, u32[]{:S(2)}) copy-start(f32[64]{0:T(128)} %copy-done.38) | copy-start | bytes 772 | tf_op jit(solution)/shard_map/while
  317.0 6.9 collective-permute-start
  344.0 26.4 %copy-start.39 = (f32[64]{0:T(128)S(1)}, f32[64]{0:T(128)}, u32[]{:S(2)}) copy-start(f32[64]{0:T(128)} %copy-done.38) | copy-start | bytes 772 | tf_op jit(solution)/shard_map/while
  364.5 6.9 collective-permute-start
  399.8 54.0 %copy-start.3 = (f32[62,2304]{1,0:T(8,128)}, f32[62,2304]{1,0:T(8,128)S(1)}, u32[]{:S(2)}) copy-start(f32[62,2304]{1,0:T(8,128)S(1)} %slice.394) | copy-start | bytes 1714180 | tf_op jit(solution)/shard_map/while
  453.8 25.8 %copy-start.6 = (f32[2,32,32]{1,2,0:T(8,128)S(1)}, f32[2,32,32]{1,2,0:T(8,128)}, u32[]{:S(2)}) copy-start(f32[2,32,32]{1,2,0:T(8,128)} %copy.214) | copy-start | bytes 24580 | tf_op jit(solution)/shard_map/while
  453.8 32.6 %copy-start.8 = (f32[64,32]{1,0:T(8,128)S(1)}, f32[64,32]{1,0:T(8,128)}, u32[]{:S(2)}) copy-start(f32[64,32]{1,0:T(8,128)} %copy-done.7) | copy-start | bytes 24580 | tf_op jit(solution)/shard_map/while
  453.8 34.9 %copy-start.5 = (f32[64,128]{1,0:T(8,128)S(1)}, f32[64,128]{1,0:T(8,128)}, u32[]{:S(2)}) copy-start(f32[64,128]{1,0:T(8,128)} %get-tuple-element.1912) | copy-start | bytes 98308 | tf_op jit(solution)/shard_map/while
  453.9 35.9 %copy-start.4 = (f32[64,128]{1,0:T(8,128)S(1)}, f32[64,128]{1,0:T(8,128)}, u32[]{:S(2)}) copy-start(f32[64,128]{1,0:T(8,128)} %get-tuple-element.1916) | copy-start | bytes 98308 | tf_op jit(solution)/shard_map/while
  483.1 30.8 %copy-start.35 = (f32[1024]{0:T(1024)S(1)}, f32[1024]{0:T(1024)}, u32[]{:S(2)}) copy-start(f32[1024]{0:T(1024)} %get-tuple-element.2088) | copy-start | bytes 12292 | tf_op jit(solution)/shard_map/while
  509.7 11.9 collective-permute-start.1
  525.0 54.0 %copy-start.3 = (f32[62,2304]{1,0:T(8,128)}, f32[62,2304]{1,0:T(8,128)S(1)}, u32[]{:S(2)}) copy-start(f32[62,2304]{1,0:T(8,128)S(1)} %slice.394) | copy-start | bytes 1714180 | tf_op jit(solution)/shard_map/while
  579.1 25.8 %copy-start.6 = (f32[2,32,32]{1,2,0:T(8,128)S(1)}, f32[2,32,32]{1,2,0:T(8,128)}, u32[]{:S(2)}) copy-start(f32[2,32,32]{1,2,0:T(8,128)} %copy.214) | copy-start | bytes 24580 | tf_op jit(solution)/shard_map/while
  579.1 32.6 %copy-start.8 = (f32[64,32]{1,0:T(8,128)S(1)}, f32[64,32]{1,0:T(8,128)}, u32[]{:S(2)}) copy-start(f32[64,32]{1,0:T(8,128)} %copy-done.7) | copy-start | bytes 24580 | tf_op jit(solution)/shard_map/while
  579.1 34.9 %copy-start.5 = (f32[64,128]{1,0:T(8,128)S(1)}, f32[64,128]{1,0:T(8,128)}, u32[]{:S(2)}) copy-start(f32[64,128]{1,0:T(8,128)} %get-tuple-element.1912) | copy-start | bytes 98308 | tf_op jit(solution)/shard_map/while
  579.1 35.9 %copy-start.4 = (f32[64,128]{1,0:T(8,128)S(1)}, f32[64,128]{1,0:T(8,128)}, u32[]{:S(2)}) copy-start(f32[64,128]{1,0:T(8,128)} %get-tuple-element.1916) | copy-start | bytes 98308 | tf_op jit(solution)/shard_map/while
  608.4 30.8 %copy-start.35 = (f32[1024]{0:T(1024)S(1)}, f32[1024]{0:T(1024)}, u32[]{:S(2)}) copy-start(f32[1024]{0:T(1024)} %get-tuple-element.2088) | copy-start | bytes 12292 | tf_op jit(solution)/shard_map/while
  635.0 14.1 %collective-permute-start.1 = (bf16[64,1024]{1,0:T(8,128)(2,1)S(1)}, bf16[64,1024]{1,0:T(8,128)(2,1)S(1)}, u32[]{:S(2)}, u32[]{:S(2)}) collective-permute-start(bf16[64,1024]{1,0:T(8,128)(2,1)S(1)} %get-tuple-element.1942), channel_id=1, source_target_pairs={{16,0},{17,1},{18,2},{19,3},{20,4},{21,5},{22,6},{23,7},{24,8},{25... | collective-permute-start | bytes 393224 | tf_op jit(solution)/shard_map/while/body/eval_jaxpr/ppermute | solution.py:13
  652.4 54.0 %copy-start.3 = (f32[62,2304]{1,0:T(8,128)}, f32[62,2304]{1,0:T(8,128)S(1)}, u32[]{:S(2)}) copy-start(f32[62,2304]{1,0:T(8,128)S(1)} %slice.394) | copy-start | bytes 1714180 | tf_op jit(solution)/shard_map/while
  706.5 25.8 %copy-start.6 = (f32[2,32,32]{1,2,0:T(8,128)S(1)}, f32[2,32,32]{1,2,0:T(8,128)}, u32[]{:S(2)}) copy-start(f32[2,32,32]{1,2,0:T(8,128)} %copy.214) | copy-start | bytes 24580 | tf_op jit(solution)/shard_map/while
  706.5 32.6 %copy-start.8 = (f32[64,32]{1,0:T(8,128)S(1)}, f32[64,32]{1,0:T(8,128)}, u32[]{:S(2)}) copy-start(f32[64,32]{1,0:T(8,128)} %copy-done.7) | copy-start | bytes 24580 | tf_op jit(solution)/shard_map/while
  706.5 34.9 %copy-start.5 = (f32[64,128]{1,0:T(8,128)S(1)}, f32[64,128]{1,0:T(8,128)}, u32[]{:S(2)}) copy-start(f32[64,128]{1,0:T(8,128)} %get-tuple-element.1912) | copy-start | bytes 98308 | tf_op jit(solution)/shard_map/while
  706.5 35.9 %copy-start.4 = (f32[64,128]{1,0:T(8,128)S(1)}, f32[64,128]{1,0:T(8,128)}, u32[]{:S(2)}) copy-start(f32[64,128]{1,0:T(8,128)} %get-tuple-element.1916) | copy-start | bytes 98308 | tf_op jit(solution)/shard_map/while
  735.8 30.7 %copy-start.35 = (f32[1024]{0:T(1024)S(1)}, f32[1024]{0:T(1024)}, u32[]{:S(2)}) copy-start(f32[1024]{0:T(1024)} %get-tuple-element.2088) | copy-start | bytes 12292 | tf_op jit(solution)/shard_map/while
  762.3 14.0 %collective-permute-start.1 = (bf16[64,1024]{1,0:T(8,128)(2,1)S(1)}, bf16[64,1024]{1,0:T(8,128)(2,1)S(1)}, u32[]{:S(2)}, u32[]{:S(2)}) collective-permute-start(bf16[64,1024]{1,0:T(8,128)(2,1)S(1)} %get-tuple-element.1942), channel_id=1, source_target_pairs={{16,0},{17,1},{18,2},{19,3},{20,4},{21,5},{22,6},{23,7},{24,8},{25... | collective-permute-start | bytes 393224 | tf_op jit(solution)/shard_map/while/body/eval_jaxpr/ppermute | solution.py:13
  779.7 54.0 %copy-start.3 = (f32[62,2304]{1,0:T(8,128)}, f32[62,2304]{1,0:T(8,128)S(1)}, u32[]{:S(2)}) copy-start(f32[62,2304]{1,0:T(8,128)S(1)} %slice.394) | copy-start | bytes 1714180 | tf_op jit(solution)/shard_map/while
  833.8 25.8 %copy-start.6 = (f32[2,32,32]{1,2,0:T(8,128)S(1)}, f32[2,32,32]{1,2,0:T(8,128)}, u32[]{:S(2)}) copy-start(f32[2,32,32]{1,2,0:T(8,128)} %copy.214) | copy-start | bytes 24580 | tf_op jit(solution)/shard_map/while
  833.8 32.6 %copy-start.8 = (f32[64,32]{1,0:T(8,128)S(1)}, f32[64,32]{1,0:T(8,128)}, u32[]{:S(2)}) copy-start(f32[64,32]{1,0:T(8,128)} %copy-done.7) | copy-start | bytes 24580 | tf_op jit(solution)/shard_map/while
  833.8 34.9 %copy-start.5 = (f32[64,128]{1,0:T(8,128)S(1)}, f32[64,128]{1,0:T(8,128)}, u32[]{:S(2)}) copy-start(f32[64,128]{1,0:T(8,128)} %get-tuple-element.1912) | copy-start | bytes 98308 | tf_op jit(solution)/shard_map/while
  833.8 35.9 %copy-start.4 = (f32[64,128]{1,0:T(8,128)S(1)}, f32[64,128]{1,0:T(8,128)}, u32[]{:S(2)}) copy-start(f32[64,128]{1,0:T(8,128)} %get-tuple-element.1916) | copy-start | bytes 98308 | tf_op jit(solution)/shard_map/while
  863.1 30.7 %copy-start.35 = (f32[1024]{0:T(1024)S(1)}, f32[1024]{0:T(1024)}, u32[]{:S(2)}) copy-start(f32[1024]{0:T(1024)} %get-tuple-element.2088) | copy-start | bytes 12292 | tf_op jit(solution)/shard_map/while
  889.6 14.1 %collective-permute-start.1 = (bf16[64,1024]{1,0:T(8,128)(2,1)S(1)}, bf16[64,1024]{1,0:T(8,128)(2,1)S(1)}, u32[]{:S(2)}, u32[]{:S(2)}) collective-permute-start(bf16[64,1024]{1,0:T(8,128)(2,1)S(1)} %get-tuple-element.1942), channel_id=1, source_target_pairs={{16,0},{17,1},{18,2},{19,3},{20,4},{21,5},{22,6},{23,7},{24,8},{25... | collective-permute-start | bytes 393224 | tf_op jit(solution)/shard_map/while/body/eval_jaxpr/ppermute | solution.py:13
  910.0 315.9 %reduce-scatter.3.cloned.1.call-start = ((), (), s32[]{:S(2)}) async-start(), calls=%async_computation.4 | async-start | bytes 19496960 | tf_op jit(solution)/shard_map/reduce_scatter | solution.py:229
  910.1 82.8 %copy-start.13 = (f32[4,64,1024]{2,1,0:T(8,128)S(1)}, f32[4,64,1024]{2,1,0:T(8,128)}, u32[]{:S(2)}) copy-start(f32[4,64,1024]{2,1,0:T(8,128)} %get-tuple-element.969) | copy-start | bytes 3145732
  910.1 82.8 %copy-start.14 = (f32[4,64,1024]{2,1,0:T(8,128)S(1)}, f32[4,64,1024]{2,1,0:T(8,128)}, u32[]{:S(2)}) copy-start(f32[4,64,1024]{2,1,0:T(8,128)} %get-tuple-element.964) | copy-start | bytes 3145732
  (82 other events, 590.2 us)
Sparse Core Ops, SparseCore 0:
  10.2 74.6 all-gather.2
  114.0 91.6 all-gather.4
  910.1 121.6 reduce-scatter.4
  1036.5 189.3 reduce-scatter.2
